TPU v7x, 256 devices: a whole 4x4x8 slice. The times are simulated.
256 devices in a mesh: ctx: 16 (over y, x), dp: 16 (over z, core).
Axes of the slice: x: 4, y: 4, z: 8, core: 2. Of those that a mesh axis runs over, the one named last changes fastest.
Arguments:
- queries: bfloat16 [16, 4096, 4096], P('dp', 'ctx'), may hold values from -6 to 6
- key_states: bfloat16 [16, 4096, 512], P('dp', 'ctx'), may hold values from -6 to 6
- value_states: bfloat16 [16, 4096, 512], P('dp', 'ctx'), may hold values from -6 to 6
- targets: bfloat16 [16, 4096, 4096], P('dp', 'ctx'), may hold values from -32 to 32
- doc_blocks: int32 [16, 8], P('dp'), may hold values from 1 to 6, 32 in all within a row
- doc_domain: int32 [16, 8], P('dp'), may hold values from 0 to 21
- domain_weight: float32 [22], replicated, may hold values from 0.25 to 4
Outputs:
- grad_queries: bfloat16 [16, 4096, 4096], P('dp', 'ctx')
- grad_keys: bfloat16 [16, 4096, 512], P('dp', 'ctx')
- grad_values: bfloat16 [16, 4096, 512], P('dp', 'ctx')
- domain_loss: float32 [22], replicated
Inputs may be any that keep to these rules, and one draw needn't show every extreme that they name: `doc_blocks`: A slab's documents take whole blocks of 128 rows, fill its 4096 rows exactly, and some document takes 6 blocks.
All inputs are finite; a program needn't handle non-finite values.
Results may differ from a plain program's by a relative error of at most 0.015.
Values may be sent and summed in bfloat16 or wider, within the bound.
A program may use at most 64 MiB of HBM per device.

v0:
```python
import jax
import jax.numpy as jnp
from jax import lax
from jax.sharding import PartitionSpec as P

HD = 128
BLOCK = 128
MOST = 6
DOMAINS = 22


def doc_index(positions, blocks_row):
    ends = jnp.cumsum(blocks_row) * BLOCK
    found = jnp.sum((positions[:, None] >= ends[None, :]).astype(jnp.int32), axis=1)
    return jnp.where(positions < 0, -1, found)


def token_domain(docs, domain_row):
    doc_count = domain_row.shape[0]
    picked = jnp.where(
        docs[:, None] == jnp.arange(doc_count, dtype=jnp.int32)[None, :], domain_row[None, :], 0
    )
    return jnp.sum(picked, axis=1)


def token_weight(domains, domain_weight):
    belongs = domains[:, None] == jnp.arange(DOMAINS, dtype=jnp.int32)[None, :]
    return jnp.sum(jnp.where(belongs, domain_weight[None, :], 0.0), axis=1)


def domain_sums(domains, token_loss):
    belongs = domains[:, None] == jnp.arange(DOMAINS, dtype=jnp.int32)[None, :]
    return jnp.sum(jnp.where(belongs, token_loss[:, None], 0.0), axis=0)


def domain_counts(domains):
    belongs = domains[:, None] == jnp.arange(DOMAINS, dtype=jnp.int32)[None, :]
    return jnp.sum(belongs.astype(jnp.float32), axis=0)


def attend(
    query_blk, key_win, value_win, target_blk, row_weight, query_pos, key_pos, query_doc, key_doc
):
    scaling = HD ** (-0.5)
    f32 = jnp.float32
    scores = jnp.einsum("qhgd,whd->hgqw", query_blk, key_win, preferred_element_type=f32) * scaling
    visible = (
        (query_doc[:, None] == key_doc[None, :])
        & (key_pos[None, :] <= query_pos[:, None])
        & (key_doc[None, :] >= 0)
    )
    scores = jnp.where(visible, scores, -1e30)
    row_max = jnp.max(scores, axis=-1, keepdims=True)
    raised = jnp.where(visible, jnp.exp(scores - row_max), 0.0)
    weights = raised / jnp.sum(raised, axis=-1, keepdims=True)
    weights_low = weights.astype(jnp.bfloat16)
    attn_out = jnp.einsum("hgqw,whd->qhgd", weights_low, value_win, preferred_element_type=f32)
    error_term = attn_out - target_blk.astype(f32)
    token_loss = 0.5 * jnp.sum(error_term * error_term, axis=(1, 2, 3))
    grad_out = (row_weight[:, None, None, None] * error_term).astype(jnp.bfloat16)
    grad_value = jnp.einsum("hgqw,qhgd->whd", weights_low, grad_out, preferred_element_type=f32)
    grad_weights = jnp.einsum("qhgd,whd->hgqw", grad_out, value_win, preferred_element_type=f32)
    center = jnp.einsum("qhgd,qhgd->hgq", grad_out.astype(f32), attn_out)
    grad_scores = (weights * (grad_weights - center[..., None])).astype(jnp.bfloat16)
    grad_query = (
        jnp.einsum("hgqw,whd->qhgd", grad_scores, key_win, preferred_element_type=f32) * scaling
    )
    grad_key = (
        jnp.einsum("hgqw,qhgd->whd", grad_scores, query_blk, preferred_element_type=f32) * scaling
    )
    return (token_loss, grad_query, grad_key, grad_value)


def on_device(queries, key_states, value_states, targets, doc_blocks, doc_domain, domain_weight):
    tok_rows = queries.shape[1]
    q_width = queries.shape[2]
    kv_width = key_states.shape[2]
    q_heads = q_width // HD
    kv_heads = kv_width // HD
    ctx_size = lax.axis_size("ctx")
    shard_index = lax.axis_index("ctx")
    blocks_row = doc_blocks[0]
    domain_row = doc_domain[0]
    pad_rows = (MOST - 1) * BLOCK
    own_pos = shard_index * tok_rows + jnp.arange(tok_rows, dtype=jnp.int32)
    own_docs = doc_index(own_pos, blocks_row)
    own_domains = token_domain(own_docs, domain_row)
    local_heads = q_heads // ctx_size
    repeat_count = ctx_size // kv_heads
    slab_rows = ctx_size * tok_rows
    query_send = queries[0].reshape(tok_rows, ctx_size, local_heads * HD)
    target_send = targets[0].reshape(tok_rows, ctx_size, local_heads * HD)
    key_rep = jnp.repeat(key_states[0].reshape(tok_rows, kv_heads, HD), repeat_count, axis=1)
    value_rep = jnp.repeat(value_states[0].reshape(tok_rows, kv_heads, HD), repeat_count, axis=1)
    pair_send = jnp.concatenate([key_rep, value_rep], axis=2)
    query_all, target_all, pair_all = (
        lax.all_to_all(query_send, "ctx", split_axis=1, concat_axis=0, tiled=True),
        lax.all_to_all(target_send, "ctx", split_axis=1, concat_axis=0, tiled=True),
        lax.all_to_all(pair_send, "ctx", split_axis=1, concat_axis=0, tiled=True),
    )
    query_all = query_all.reshape(slab_rows, 1, local_heads, HD)
    target_all = target_all.reshape(slab_rows, 1, local_heads, HD)
    key_all = pair_all[:, 0, :HD].reshape(slab_rows, 1, HD)
    value_all = pair_all[:, 0, HD:].reshape(slab_rows, 1, HD)
    positions = jnp.arange(slab_rows, dtype=jnp.int32)
    slab_docs = doc_index(positions, blocks_row)
    slab_domains = token_domain(slab_docs, domain_row)
    slab_weight = token_weight(slab_domains, domain_weight)
    block_rows = min(512, slab_rows)
    window_rows = pad_rows + block_rows
    key_pad = jnp.concatenate([jnp.zeros((pad_rows, 1, HD), jnp.bfloat16), key_all], axis=0)
    value_pad = jnp.concatenate([jnp.zeros((pad_rows, 1, HD), jnp.bfloat16), value_all], axis=0)
    pad_pos = jnp.arange(-pad_rows, slab_rows, dtype=jnp.int32)
    pad_docs = doc_index(pad_pos, blocks_row)

    def block_step(running, block_id):
        key_acc, value_acc = running
        first_row = block_id * block_rows
        token_loss, grad_query, grad_key, grad_value = attend(
            lax.dynamic_slice_in_dim(query_all, first_row, block_rows, 0),
            lax.dynamic_slice_in_dim(key_pad, first_row, window_rows, 0),
            lax.dynamic_slice_in_dim(value_pad, first_row, window_rows, 0),
            lax.dynamic_slice_in_dim(target_all, first_row, block_rows, 0),
            lax.dynamic_slice_in_dim(slab_weight, first_row, block_rows, 0),
            lax.dynamic_slice_in_dim(positions, first_row, block_rows, 0),
            lax.dynamic_slice_in_dim(pad_pos, first_row, window_rows, 0),
            lax.dynamic_slice_in_dim(slab_docs, first_row, block_rows, 0),
            lax.dynamic_slice_in_dim(pad_docs, first_row, window_rows, 0),
        )
        key_acc = lax.dynamic_update_slice_in_dim(
            key_acc,
            lax.dynamic_slice_in_dim(key_acc, first_row, window_rows, 0) + grad_key,
            first_row,
            0,
        )
        value_acc = lax.dynamic_update_slice_in_dim(
            value_acc,
            lax.dynamic_slice_in_dim(value_acc, first_row, window_rows, 0) + grad_value,
            first_row,
            0,
        )
        return ((key_acc, value_acc), (token_loss, grad_query))

    zero_acc = jnp.zeros((pad_rows + slab_rows, 1, HD), jnp.float32)
    (key_acc, value_acc), (block_loss, block_query) = lax.scan(
        block_step, (zero_acc, zero_acc), jnp.arange(slab_rows // block_rows, dtype=jnp.int32)
    )
    query_back = block_query.reshape(slab_rows, 1, local_heads * HD).astype(jnp.bfloat16)
    grad_q = lax.all_to_all(query_back, "ctx", split_axis=0, concat_axis=1, tiled=True).reshape(
        tok_rows, q_width
    )
    pair_grad = jnp.concatenate([key_acc[pad_rows:], value_acc[pad_rows:]], axis=2)
    pair_back = lax.all_to_all(pair_grad, "ctx", split_axis=0, concat_axis=1, tiled=True)
    pair_sum = jnp.sum(pair_back.reshape(tok_rows, kv_heads, repeat_count, 2 * HD), axis=2)
    grad_k = pair_sum[:, :, :HD].reshape(tok_rows, kv_width).astype(jnp.bfloat16)
    grad_v = pair_sum[:, :, HD:].reshape(tok_rows, kv_width).astype(jnp.bfloat16)
    loss_sums = domain_sums(slab_domains, block_loss.reshape(slab_rows))
    row_counts = domain_counts(own_domains)
    totals, tallies = lax.psum((loss_sums, row_counts), ("ctx", "dp"))
    domain_loss = totals / (jnp.maximum(tallies, 1.0) * (q_heads * HD))
    return (grad_q[None], grad_k[None], grad_v[None], domain_loss)


def solution(mesh):
    placed = (
        P("dp", "ctx", None),
        P("dp", "ctx", None),
        P("dp", "ctx", None),
        P("dp", "ctx", None),
        P("dp", None),
        P("dp", None),
        P(),
    )
    return jax.shard_map(
        on_device,
        mesh=mesh,
        in_specs=placed,
        out_specs=(P("dp", "ctx", None), P("dp", "ctx", None), P("dp", "ctx", None), P()),
        check_vma=False,
    )
```

profile of v0, /device:TPU:24, one launch (start us, length us, event | category | flops | bytes accessed | tf_op | source)
XLA Modules:
  0.0 520.0 jit_solution(1308710611630207780)
XLA Ops:
  4.5 7.2 %all-to-all-start.1 = ((bf16[256,16,256]{0,2,1:T(8,128)(2,1)}), bf16[256,16,256]{0,2,1:T(8,128)(2,1)S(1)}, u32[]{:S(2)}, u32[]{:S(2)}) async-start(bf16[256,16,256]{0,2,1:T(8,128)(2,1)} %pad_maximum_fusion.1), calls=%async_computation.1 | async-start | bytes 4194304 | tf_op jit(solution)/shard_map/all_to_all | solution.py:99
  11.7 4.1 copy.115
  15.8 26.3 %all-to-all-done.1 = bf16[256,16,256]{0,2,1:T(8,128)(2,1)S(1)} async-done(((bf16[256,16,256]{0,2,1:T(8,128)(2,1)}), bf16[256,16,256]{0,2,1:T(8,128)(2,1)S(1)}, u32[]{:S(2)}, u32[]{:S(2)}) %all-to-all-start.1) | async-done | bytes 2097184 | tf_op jit(solution)/shard_map/all_to_all | solution.py:99
  43.4 5.1 all-to-all-start
  48.7 4.1 copy.120
  52.8 24.4 %all-to-all-done = bf16[256,16,256]{0,2,1:T(8,128)(2,1)S(1)} async-done(((bf16[256,16,256]{0,2,1:T(8,128)(2,1)}), bf16[256,16,256]{0,2,1:T(8,128)(2,1)S(1)}, u32[]{:S(2)}, u32[]{:S(2)}) %all-to-all-start) | async-done | bytes 2097184 | tf_op jit(solution)/shard_map/all_to_all | solution.py:97
  77.2 5.8 %all-to-all-start.2 = ((bf16[256,16,256]{0,2,1:T(8,128)(2,1)}), bf16[256,16,256]{0,2,1:T(8,128)(2,1)}, u32[]{:S(2)}, u32[]{:S(2)}) async-start(bf16[256,16,256]{0,2,1:T(8,128)(2,1)} %bitcast.241), calls=%async_computation.2 | async-start | bytes 4194304 | tf_op jit(solution)/shard_map/all_to_all | solution.py:98
  83.8 3.9 copy.119
  94.3 4.2 reshape.186
  98.5 12.6 %all-to-all-done.2 = bf16[256,16,256]{0,2,1:T(8,128)(2,1)} async-done(((bf16[256,16,256]{0,2,1:T(8,128)(2,1)}), bf16[256,16,256]{0,2,1:T(8,128)(2,1)}, u32[]{:S(2)}, u32[]{:S(2)}) %all-to-all-start.2) | async-done | bytes 2097184 | tf_op jit(solution)/shard_map/all_to_all | solution.py:98
  111.0 2.8 copy.121
  118.0 163.2 %while.16 = (s32[]{:T(128)}, f32[4736,1,128]{0,2,1:T(8,128)S(1)}, f32[4736,1,128]{0,2,1:T(8,128)}, f32[8,512]{1,0:T(8,128)S(1)}, bf16[8,512,1,2,128]{1,4,3,2,0:T...) while((s32[]{:T(128)}, f32[4736,1,128]{0,2,1:T(8,128)S(1)}, ...), condition=%wide.region_9.10_spmd, body=%wide.region_5.9_spmd.sunk | while | flops 1844623488 | bytes 41261128 | solution.py:145
  126.7 3.6 fusion.72
  130.3 2.8 fusion.70
  144.4 2.7 fusion.69
  147.1 3.6 fusion.72
  150.7 2.8 fusion.70
  164.8 2.7 fusion.69
  167.5 3.6 fusion.72
  171.1 2.8 fusion.70
  185.2 2.7 fusion.69
  187.9 3.7 fusion.72
  191.5 2.8 fusion.70
  205.6 2.7 fusion.69
  208.3 3.7 fusion.72
  212.0 2.8 fusion.70
  226.1 2.7 fusion.69
  228.8 3.6 fusion.72
  232.5 2.8 fusion.70
  246.5 2.7 fusion.69
  249.2 3.6 fusion.72
  252.8 2.8 fusion.70
  266.9 2.7 fusion.69
  269.6 3.6 fusion.72
  273.2 2.8 fusion.70
  281.2 6.2 %copy.154 = bf16[8,512,1,2,128]{4,3,1,0,2:T(2,128)(2,1)} copy(bf16[8,512,1,2,128]{1,4,3,2,0:T(8,128)(2,1)} %get-tuple-element.84) | data formatting | bytes 4194304 | tf_op jit(solution)/shard_map/convert_element_type | solution.py:148
  287.4 13.5 %reshape.201 = bf16[4096,1,256]{2,1,0:T(2,128)(2,1)} reshape(bf16[8,512,1,2,128]{4,3,1,0,2:T(2,128)(2,1)} %copy.154) | data formatting | bytes 4194304 | tf_op jit(solution)/shard_map/convert_element_type | solution.py:148
  301.5 23.1 %reduce.4 = bf16[4096,256]{1,0:T(8,128)(2,1)} reduce(bf16[4096,1,256]{2,1,0:T(2,128)(2,1)} %reshape.201, bf16[]{:T(256)} %broadcast.105), dimensions={1}, to_apply=%reshape.201.reduce_sub_computation | reduce | bytes 4194306 | tf_op jit(solution)/shard_map/convert_element_type | solution.py:148
  324.6 4.0 reshape.203
  328.6 6.0 %all-to-all-start.3 = ((bf16[16,2,32768]{2,1,0:T(2,128)(2,1)}), bf16[16,2,32768]{2,1,0:T(2,128)(2,1)}, u32[]{:S(2)}, u32[]{:S(2)}) async-start(bf16[16,2,32768]{2,1,0:T(2,128)(2,1)} %reshape.203), calls=%async_computation.3 | async-start | bytes 4194304 | tf_op jit(solution)/shard_map/all_to_all | solution.py:149
  336.1 5.8 %copy.127 = f32[4096,1,128]{2,1,0:T(1,128)} copy(f32[4096,1,128]{0,2,1:T(8,128)} %slice.22) | data formatting | bytes 4194304 | tf_op jit(solution)/shard_map/slice | solution.py:152
  343.4 5.8 %copy.128 = f32[4096,1,128]{2,1,0:T(1,128)} copy(f32[4096,1,128]{0,2,1:T(8,128)} %slice.23) | data formatting | bytes 4194304 | tf_op jit(solution)/shard_map/slice | solution.py:152
  349.2 7.7 %pad_maximum_fusion = f32[4096,1,256]{2,1,0:T(1,128)} fusion(f32[4096,1,128]{2,1,0:T(1,128)} %copy.128, f32[4096,1,128]{2,1,0:T(1,128)S(1)} %copy-done.2), kind=kLoop, calls=%fused_computation.52 | loop fusion | flops 1048576 | bytes 8388608 | tf_op jit(solution)/shard_map/concatenate | solution.py:152
  356.9 5.3 %all-to-all-done.3 = bf16[16,2,32768]{2,1,0:T(2,128)(2,1)} async-done(((bf16[16,2,32768]{2,1,0:T(2,128)(2,1)}), bf16[16,2,32768]{2,1,0:T(2,128)(2,1)}, u32[]{:S(2)}, u32[]{:S(2)}) %all-to-all-start.3) | async-done | bytes 2097184 | tf_op jit(solution)/shard_map/all_to_all | solution.py:149
  362.1 6.2 %all-to-all-start.4 = ((f32[4096,1,256]{2,1,0:T(1,128)}), f32[4096,1,256]{2,1,0:T(1,128)}, u32[]{:S(2)}, u32[]{:S(2)}) async-start(f32[4096,1,256]{2,1,0:T(1,128)} %pad_maximum_fusion), calls=%async_computation.4 | async-start | bytes 8388608 | tf_op jit(solution)/shard_map/all_to_all | solution.py:153
  368.9 125.9 %all-reduce.2 = (f32[22]{0:T(128)S(1)}, f32[22]{0:T(128)S(1)}) all-reduce(f32[22]{0:T(128)S(1)} %select_reduce_fusion, f32[22]{0:T(128)S(1)} %convert_reduce_fusion.2), channel_id=1, replica_groups=mesh['ctx'=16,'dp'=16] {'ctx','dp'}, use_global_device_ids=true, to_apply=%region_12.13 | all-reduce | flops 44 | bytes 352 | tf_op jit(solution)/shard_map/psum | solution.py:159
  495.3 10.5 %reshape.204 = bf16[4096,1,256]{2,1,0:T(2,128)(2,1)} reshape(bf16[16,2,32768]{2,1,0:T(2,128)(2,1)} %all-to-all-done.3) | data formatting | bytes 4194304
  510.8 4.1 copy.132
  (181 shorter events, 118.8 us)
Async XLA Ops:
  4.5 37.5 %all-to-all-start.1 = ((bf16[256,16,256]{0,2,1:T(8,128)(2,1)}), bf16[256,16,256]{0,2,1:T(8,128)(2,1)S(1)}, u32[]{:S(2)}, u32[]{:S(2)}) async-start(bf16[256,16,256]{0,2,1:T(8,128)(2,1)} %pad_maximum_fusion.1), calls=%async_computation.1 | async-start | bytes 4194304 | tf_op jit(solution)/shard_map/all_to_all | solution.py:99
  15.8 32.7 %copy-start.10 = (s32[1,8]{1,0:T(1,128)S(1)}, s32[1,8]{1,0:T(1,128)}, u32[]{:S(2)}) copy-start(s32[1,8]{1,0:T(1,128)} %param.13) | copy-start | bytes 100
  42.0 1.4 copy-start.1
  43.4 33.8 %all-to-all-start = ((bf16[256,16,256]{0,2,1:T(8,128)(2,1)}), bf16[256,16,256]{0,2,1:T(8,128)(2,1)S(1)}, u32[]{:S(2)}, u32[]{:S(2)}) async-start(bf16[256,16,256]{0,2,1:T(8,128)(2,1)} %bitcast.242), calls=%async_computation | async-start | bytes 4194304 | tf_op jit(solution)/shard_map/all_to_all | solution.py:97
  52.8 30.8 %copy-start.7 = (s32[1,8]{1,0:T(1,128)S(1)}, s32[1,8]{1,0:T(1,128)}, u32[]{:S(2)}) copy-start(s32[1,8]{1,0:T(1,128)} %param.14) | copy-start | bytes 100
  52.8 30.9 %copy-start.9 = (f32[22]{0:T(128)S(1)}, f32[22]{0:T(128)}, u32[]{:S(2)}) copy-start(f32[22]{0:T(128)} %param.15) | copy-start | bytes 268
  77.2 33.9 %all-to-all-start.2 = ((bf16[256,16,256]{0,2,1:T(8,128)(2,1)}), bf16[256,16,256]{0,2,1:T(8,128)(2,1)}, u32[]{:S(2)}, u32[]{:S(2)}) async-start(bf16[256,16,256]{0,2,1:T(8,128)(2,1)} %bitcast.241), calls=%async_computation.2 | async-start | bytes 4194304 | tf_op jit(solution)/shard_map/all_to_all | solution.py:98
  83.0 0.5 copy-start.5
  83.6 5.8 %copy-start.3 = (s32[4096]{0:T(1024)}, s32[4096]{0:T(1024)S(1)}, u32[]{:S(2)}) copy-start(s32[4096]{0:T(1024)S(1)} %select_reduce_fusion.2) | copy-start | bytes 49156
  328.6 33.6 %all-to-all-start.3 = ((bf16[16,2,32768]{2,1,0:T(2,128)(2,1)}), bf16[16,2,32768]{2,1,0:T(2,128)(2,1)}, u32[]{:S(2)}, u32[]{:S(2)}) async-start(bf16[16,2,32768]{2,1,0:T(2,128)(2,1)} %reshape.203), calls=%async_computation.3 | async-start | bytes 4194304 | tf_op jit(solution)/shard_map/all_to_all | solution.py:149
  336.1 5.8 %copy-start = (f32[4736,1,128]{0,2,1:T(8,128)S(1)}, f32[4736,1,128]{0,2,1:T(8,128)}, u32[]{:S(2)}) copy-start(f32[4736,1,128]{0,2,1:T(8,128)} %get-tuple-element.86) | copy-start | bytes 7274500
  343.4 5.8 %copy-start.2 = (f32[4096,1,128]{2,1,0:T(1,128)S(1)}, f32[4096,1,128]{2,1,0:T(1,128)}, u32[]{:S(2)}) copy-start(f32[4096,1,128]{2,1,0:T(1,128)} %copy.127) | copy-start | bytes 6291460
  356.9 11.5 %copy-start.6 = (s32[8]{0:T(128)S(1)}, s32[8]{0:T(128)}, u32[]{:S(2)}) copy-start(s32[8]{0:T(128)} %copy-done.5) | copy-start | bytes 100
  356.9 11.6 %copy-start.8 = (s32[1,8]{1,0:T(1,128)S(1)}, s32[1,8]{1,0:T(1,128)}, u32[]{:S(2)}) copy-start(s32[1,8]{1,0:T(1,128)} %param.14) | copy-start | bytes 100
  356.9 11.8 %copy-start.4 = (s32[4096]{0:T(1024)S(1)}, s32[4096]{0:T(1024)}, u32[]{:S(2)}) copy-start(s32[4096]{0:T(1024)} %copy-done.3) | copy-start | bytes 49156
  362.1 152.7 %all-to-all-start.4 = ((f32[4096,1,256]{2,1,0:T(1,128)}), f32[4096,1,256]{2,1,0:T(1,128)}, u32[]{:S(2)}, u32[]{:S(2)}) async-start(f32[4096,1,256]{2,1,0:T(1,128)} %pad_maximum_fusion), calls=%async_computation.4 | async-start | bytes 8388608 | tf_op jit(solution)/shard_map/all_to_all | solution.py:153
where the time goes:
time: 525 us; the launch traced here: 520 us
  blocking collectives  126 us (24%)
  matrix products  123 us (23%)
  local copies, waits for them, and re-layouts  105 us (20%)
  waiting for transfers between devices  68.5 us (13%)
  other arithmetic  61.1 us (12%)
  starting transfers between devices  30.3 us (6%)
  loops' own time  5.6 us (1%)
    psum x1, blocking collectives, on_device(): totals, tallies = lax.psum((loss_sums, row_counts), ('ctx', 'dp'))  126 us
    unnamed x33, local copies, waits for them, and re-layouts  35.5 us
    dot_general x8, matrix products, attend(): jnp.einsum('hgqw,qhgd->whd', weights_low, grad_out, preferred_element_typ...  29.1 us
    all_to_all x1, waiting for transfers between devices, on_device(): lax.all_to_all(pair_send, 'ctx', split_axis=1, concat_axis=0, tiled=True)  26.3 us
    all_to_all x1, waiting for transfers between devices, on_device(): lax.all_to_all(query_send, 'ctx', split_axis=1, concat_axis=0, tiled=True)  24.4 us
    convert_element_type x1, other arithmetic, on_device(): block_query.reshape(slab_rows, 1, local_heads * HD).astype(jnp.bfloat16)  23.1 us
    dot_general x8, matrix products, attend(): jnp.einsum('qhgd,whd->hgqw', grad_out, value_win, preferred_element_type=...  22.3 us
    dot_general x8, matrix products, attend(): jnp.einsum('hgqw,whd->qhgd', weights_low, value_win, preferred_element_ty...  21.6 us
  transfers between devices with their start and end apart: 5, of which 4 were waited for; matrix products, arithmetic and copies ran while one was open for 13% of the time, Pallas kernels for 0%

commit v1 on v0

v1 whole, which is shorter than its diff:
```python
import functools

import jax
import jax.numpy as jnp
from jax import lax
from jax.experimental import pallas as pl
from jax.experimental.pallas import tpu as pltpu
from jax.sharding import PartitionSpec as P

HD = 128
BLOCK = 128
MOST = 6
DOMAINS = 22
SCALE = HD**-0.5
LOG2E = 1.4426950408889634
HIDDEN = -1e30
HALO = (MOST - 1) * BLOCK
WINDOW = MOST * BLOCK
NT = (((1,), (1,)), ((), ()))
NN = (((1,), (0,)), ((), ()))
MESH = pl.DeviceIdType.MESH
f32 = jnp.float32
bf16 = jnp.bfloat16


def dot(a, b, dims):
    return lax.dot_general(a, b, dims, preferred_element_type=f32)


def kernel(
    n_ctx, n_dp, groups, per_group,
    blocks_ref, domain_ref, weight_ref, q_hbm, k_hbm, v_hbm, t_hbm,
    gq_hbm, gk_hbm, gv_hbm, loss_ref,
    qv, tv, gqv, kv, kT, vT, acc, own, sbuf, rbuf, outv, lossv, lsend, lrecv, tri,
    kv_sem, q_sem, t_sem, halo_send, halo_recv, grad_send, grad_recv, gq_sem, out_sem, l_send, l_recv,
):
    me = lax.axis_index("ctx")
    my_dp = lax.axis_index("dp")
    rows = 2 * BLOCK
    heads_w = per_group * HD

    def kv_copy(g, which):
        src = (k_hbm, v_hbm)[which]
        return pltpu.make_async_copy(
            src.at[:, pl.ds(pl.multiple_of(g * HD, HD), HD)],
            kv.at[g, which, pl.ds(HALO, rows), :],
            kv_sem.at[g, which],
        )

    def wide(ref, g):
        return ref.at[:, pl.ds(pl.multiple_of(g * heads_w, heads_w), heads_w)]

    def q_copy(g):
        return pltpu.make_async_copy(wide(q_hbm, g), wide(qv, g), q_sem.at[g])

    def t_copy(g):
        return pltpu.make_async_copy(wide(t_hbm, g), wide(tv, g), t_sem.at[g])

    def gq_copy(g):
        return pltpu.make_async_copy(wide(gqv, g), wide(gq_hbm, g), gq_sem.at[g])

    spans = ((1, HALO, HALO - rows, rows), (2, HALO, HALO - 2 * rows, rows), (3, HALO + BLOCK, 0, BLOCK))

    def halo_copy(g, i):
        ahead, first, there, count = spans[i]
        return pltpu.make_async_remote_copy(
            src_ref=kv.at[g, :, pl.ds(first, count), :],
            dst_ref=kv.at[g, :, pl.ds(there, count), :],
            send_sem=halo_send.at[g, i],
            recv_sem=halo_recv.at[g, i],
            device_id={"ctx": lax.rem(me + ahead, n_ctx)},
            device_id_type=MESH,
        )

    def grad_copy(g, i):
        ahead, _, there, count = spans[i]
        return pltpu.make_async_remote_copy(
            src_ref=sbuf.at[g, :, pl.ds(there, count), :],
            dst_ref=rbuf.at[g, :, pl.ds(there, count), :],
            send_sem=grad_send.at[g, i],
            recv_sem=grad_recv.at[g, i],
            device_id={"ctx": lax.rem(me + n_ctx - ahead, n_ctx)},
            device_id_type=MESH,
        )

    def out_copy(which):
        dst = (gk_hbm, gv_hbm)[which]
        return pltpu.make_async_copy(outv.at[which], dst, out_sem.at[which])

    def loss_copy(phase, i):
        if phase == 0:
            slot, target = me, {"ctx": lax.rem(me + i, n_ctx)}
        else:
            slot, target = my_dp, {"dp": lax.rem(my_dp + i, n_dp)}
        return pltpu.make_async_remote_copy(
            src_ref=lsend.at[phase],
            dst_ref=lrecv.at[phase, slot],
            send_sem=l_send.at[phase, i],
            recv_sem=l_recv.at[phase, i],
            device_id=target,
            device_id_type=MESH,
        )

    for g in range(groups):
        kv_copy(g, 0).start()
        kv_copy(g, 1).start()
    for g in range(groups):
        q_copy(g).start()
        t_copy(g).start()

    barrier = pltpu.get_barrier_semaphore()
    for i in range(1, n_ctx):
        pl.semaphore_signal(barrier, inc=1, device_id={"ctx": lax.rem(me + i, n_ctx)}, device_id_type=MESH)
    for i in range(1, n_dp):
        pl.semaphore_signal(barrier, inc=1, device_id={"dp": lax.rem(my_dp + i, n_dp)}, device_id_type=MESH)

    first_block = [2 * me, 2 * me + 1]
    doc_count = blocks_ref.shape[1]
    starts, omegas, domains = [], [], []
    for b in range(2):
        end = jnp.int32(0)
        start = jnp.int32(0)
        doc = jnp.int32(0)
        for i in range(doc_count - 1):
            end = end + blocks_ref[0, i]
            passed = first_block[b] >= end
            start = jnp.where(passed, end, start)
            doc = doc + jnp.where(passed, 1, 0)
        domain = domain_ref[0, doc]
        starts.append(start)
        domains.append(domain)
        omegas.append(weight_ref[domain])
    bias = [
        [jnp.where(first_block[b] - (MOST - 1) + j >= starts[b], 0.0, HIDDEN).astype(f32) for j in range(MOST - 1)]
        for b in range(2)
    ]
    key_row = lax.broadcasted_iota(jnp.int32, (BLOCK, heads_w), 0)
    query_col = lax.rem(lax.broadcasted_iota(jnp.int32, (BLOCK, heads_w), 1), BLOCK)
    tri[...] = jnp.where(key_row <= query_col, 0.0, HIDDEN).astype(f32)
    lossv[...] = jnp.zeros_like(lossv)

    pl.semaphore_wait(barrier, n_ctx - 1 + n_dp - 1)

    for g in range(groups):
        kv_copy(g, 0).wait()
        kv_copy(g, 1).wait()
        for i in range(3):
            halo_copy(g, i).start()

    def finish(g):
        for i in range(3):
            grad_copy(g, i).wait_recv()
        lanes = pl.ds(pl.multiple_of(g * HD, HD), HD)
        near = slice(HALO - rows, HALO)
        middle = slice(HALO - 2 * rows, HALO - rows)
        for which in range(2):
            total = own[g, which] + rbuf[g, which, near, :].astype(f32) + rbuf[g, which, middle, :].astype(f32)
            far = rbuf[g, which, 0:BLOCK, :].astype(f32)
            outv[which, 0:BLOCK, lanes] = total[0:BLOCK].astype(bf16)
            outv[which, BLOCK:rows, lanes] = (total[BLOCK:rows] + far).astype(bf16)

    def attend(g, b):
        first = BLOCK * b
        base = g * heads_w

        def columns(h):
            return pl.ds(pl.multiple_of(base + h * HD, HD), HD)

        key_win = kv[g, 0, first : first + WINDOW, :]
        value_win = kv[g, 1, first : first + WINDOW, :]
        query = jnp.concatenate([qv[first : first + BLOCK, columns(h)] for h in range(per_group)], 0)
        target = jnp.concatenate([tv[first : first + BLOCK, columns(h)].astype(f32).T for h in range(per_group)], 1)
        scores = dot(key_win, query, NT)
        parts, top = [], None
        for j in range(MOST):
            part = scores[BLOCK * j : BLOCK * (j + 1)]
            if j == MOST - 1:
                part = part + tri[...]
            parts.append(part)
            part_top = jnp.max(part.reshape(BLOCK // 8, 8, heads_w), axis=0)
            if j < MOST - 1:
                part_top = part_top + bias[b][j]
            top = part_top if top is None else jnp.maximum(top, part_top)
        shift = jnp.max(top, axis=0, keepdims=True) * (SCALE * LOG2E)
        raised, sums = [], None
        for j in range(MOST):
            off = shift if j == MOST - 1 else shift - bias[b][j]
            part = jnp.exp2(parts[j] * (SCALE * LOG2E) - off)
            raised.append(part)
            part_sum = jnp.sum(part.reshape(BLOCK // 8, 8, heads_w), axis=0)
            sums = part_sum if sums is None else sums + part_sum
        inverse = 1.0 / jnp.sum(sums, axis=0, keepdims=True)
        raised = jnp.concatenate(raised, 0)
        raised_low = raised.astype(bf16)
        out = dot(vT[:, first : first + WINDOW], raised_low, NN) * inverse
        error = out - target
        squares = error * error
        lossv[b] += jnp.sum(squares.reshape(HD // 8, 8, heads_w), axis=0)
        grad_out = (error * (inverse * omegas[b])).astype(bf16)
        center = jnp.sum(grad_out.astype(f32) * out, axis=0, keepdims=True)
        grad_probs = dot(value_win, grad_out, NN)
        grad_scores = (raised * (grad_probs - center)).astype(bf16)
        grad_query = dot(kT[:, first : first + WINDOW], grad_scores, NN) * SCALE
        for h in range(per_group):
            gqv[first : first + BLOCK, columns(h)] = grad_query[:, HD * h : HD * (h + 1)].T.astype(bf16)
        grad_value = dot(raised_low, grad_out, NT)
        grad_key = dot(grad_scores, query, NN) * SCALE
        for which, part in ((0, grad_key), (1, grad_value)):
            if b == 0:
                acc[which, 0:WINDOW, :] = part
            else:
                acc[which, BLOCK:WINDOW, :] += part[0 : WINDOW - BLOCK]
                acc[which, WINDOW:, :] = part[WINDOW - BLOCK :]

    def step(g, carry):
        for i in range(3):
            halo_copy(g, i).wait_recv()
        q_copy(g).wait()
        t_copy(g).wait()
        kT[...] = kv[g, 0].T
        vT[...] = kv[g, 1].T
        attend(g, 0)
        attend(g, 1)
        for which in range(2):
            sbuf[g, which] = acc[which, 0:HALO, :].astype(bf16)
            own[g, which] = acc[which, HALO:, :]
        for i in (2, 1, 0):
            grad_copy(g, i).start()
        gq_copy(g).start()

        @pl.when(g > 0)
        def _():
            finish(g - 1)

        return carry

    lax.fori_loop(0, groups, step, 0)

    lane = lax.broadcasted_iota(jnp.int32, (8, HD), 1)
    line = lax.broadcasted_iota(jnp.int32, (8, HD), 0)
    tile = jnp.zeros((8, HD), f32)
    for b in range(2):
        block_loss = 0.5 * jnp.sum(jnp.sum(lossv[b], axis=0, keepdims=True), axis=1, keepdims=True)
        picked = jnp.where(line == 0, block_loss, jnp.where(line == 1, float(BLOCK), 0.0))
        tile = tile + jnp.where(lane == domains[b], picked, 0.0)
    for phase in range(2):
        n = (n_ctx, n_dp)[phase]
        lsend[phase] = tile
        lrecv[phase, (me, my_dp)[phase]] = tile
        for i in range(1, n):
            loss_copy(phase, i).start()
        if phase == 0:
            finish(groups - 1)
            out_copy(0).start()
            out_copy(1).start()
        for i in range(1, n):
            loss_copy(phase, i).wait()
        tile = lrecv[phase, 0]
        for i in range(1, n):
            tile = tile + lrecv[phase, i]
    loss_ref[...] = tile[0:1] / (jnp.maximum(tile[1:2], 1.0) * float(groups * per_group * HD))

    for g in range(groups):
        for i in range(3):
            halo_copy(g, i).wait_send()
            grad_copy(g, i).wait_send()
        gq_copy(g).wait()
    out_copy(0).wait()
    out_copy(1).wait()


def on_device(n_ctx, n_dp, queries, key_states, value_states, targets, doc_blocks, doc_domain, domain_weight):
    rows, q_width = queries.shape[1:]
    kv_width = key_states.shape[2]
    groups = kv_width // HD
    per_group = q_width // kv_width
    heads_w = per_group * HD
    any_space = pl.BlockSpec(memory_space=pl.ANY)
    smem = pl.BlockSpec(memory_space=pltpu.SMEM)
    dma = pltpu.SemaphoreType.DMA
    span = HALO + rows
    most_peers = max(n_ctx, n_dp)
    gq, gk, gv, loss = pl.pallas_call(
        functools.partial(kernel, n_ctx, n_dp, groups, per_group),
        out_shape=(
            jax.ShapeDtypeStruct((rows, q_width), bf16),
            jax.ShapeDtypeStruct((rows, kv_width), bf16),
            jax.ShapeDtypeStruct((rows, kv_width), bf16),
            jax.ShapeDtypeStruct((1, HD), f32),
        ),
        in_specs=[smem, smem, smem, any_space, any_space, any_space, any_space],
        out_specs=(any_space, any_space, any_space, pl.BlockSpec(memory_space=pltpu.VMEM)),
        scratch_shapes=[
            pltpu.VMEM((rows, q_width), bf16),
            pltpu.VMEM((rows, q_width), bf16),
            pltpu.VMEM((rows, q_width), bf16),
            pltpu.VMEM((groups, 2, span, HD), bf16),
            pltpu.VMEM((HD, span), bf16),
            pltpu.VMEM((HD, span), bf16),
            pltpu.VMEM((2, span, HD), f32),
            pltpu.VMEM((groups, 2, rows, HD), f32),
            pltpu.VMEM((groups, 2, HALO, HD), bf16),
            pltpu.VMEM((groups, 2, HALO, HD), bf16),
            pltpu.VMEM((2, rows, kv_width), bf16),
            pltpu.VMEM((2, 8, heads_w), f32),
            pltpu.VMEM((2, 8, HD), f32),
            pltpu.VMEM((2, most_peers, 8, HD), f32),
            pltpu.VMEM((BLOCK, heads_w), f32),
            dma((groups, 2)),
            dma((groups,)),
            dma((groups,)),
            dma((groups, 3)),
            dma((groups, 3)),
            dma((groups, 3)),
            dma((groups, 3)),
            dma((groups,)),
            dma((2,)),
            dma((2, most_peers)),
            dma((2, most_peers)),
        ],
        compiler_params=pltpu.CompilerParams(collective_id=0, has_side_effects=True, vmem_limit_bytes=60 << 20),
    )(doc_blocks, doc_domain, domain_weight, queries[0], key_states[0], value_states[0], targets[0])
    return gq[None], gk[None], gv[None], loss[0, :DOMAINS]


def solution(mesh):
    placed = (
        P("dp", "ctx", None),
        P("dp", "ctx", None),
        P("dp", "ctx", None),
        P("dp", "ctx", None),
        P("dp", None),
        P("dp", None),
        P(),
    )
    return jax.shard_map(
        functools.partial(on_device, mesh.shape["ctx"], mesh.shape["dp"]),
        mesh=mesh,
        in_specs=placed,
        out_specs=(P("dp", "ctx", None), P("dp", "ctx", None), P("dp", "ctx", None), P()),
        check_vma=False,
    )
```

time: 525 us -> 81.9 us (0.16)
  the two profiles are of different devices: /device:TPU:24 before, /device:TPU:1 now
where the time goes in v1:
time: 81.9 us; the launch traced here: 81.7 us
  Pallas kernels  75.3 us (92%)
  local copies, waits for them, and re-layouts  5.77 us (7%)
    pallas_call x1, Pallas kernels, on_device(): pl.pallas_call(functools.partial(kernel, n_ctx, n_dp, groups, per_group),...  75.3 us
    unnamed x7, local copies, waits for them, and re-layouts  4.6 us

profile of v1, /device:TPU:1, one launch (start us, length us, event | category | flops | bytes accessed | tf_op | source)
XLA Modules:
  0.0 81.7 jit_solution(7214570016408133130)
XLA Ops:
  0.6 75.3 %shard_map.102 = (bf16[256,4096]{1,0:T(8,128)(2,1)}, bf16[256,512]{1,0:T(8,128)(2,1)}, bf16[256,512]{1,0:T(8,128)(2,1)}, f32[1,128]{1,0:T(1,128)}) custom-call(s32[1,8]{1,0:T(1,128)} %blocks_ref.1, s32[1,8]{1,0:T(1,128)} %domain_ref.1, f32[22]{0:T(128)} %weight_ref.1, bf16[256,4096]{1,0:T(8,128)(2,1)} %bitcast.9, bf16[256,512]{1,0:T(8,128)(2,1)} %bitcast.12, ...), custom_call_target="tpu_custom_call" | custom-call | tf_op jit(solution)/shard_map/pallas_call | solution.py:283
  76.0 1.2 %slice_bitcast_fusion = f32[22]{0:T(128)} fusion(f32[1,128]{1,0:T(1,128)} %get-tuple-element.11), kind=kLoop, calls=%fused_computation | loop fusion | bytes 176 | tf_op jit(solution)/shard_map/squeeze | solution.py:323
  77.1 0.0 copy-start.1
  77.1 0.0 copy-start
  77.1 3.2 %copy.14 = bf16[1,256,4096]{2,1,0:T(8,128)(2,1)} copy(bf16[1,256,4096]{2,1,0:T(8,128)(2,1)} %bitcast.11) | data formatting | bytes 4194304
  80.3 0.0 copy-done.1
  80.3 0.7 copy.15
  81.0 0.0 copy-done
  81.0 0.7 copy.16
Async XLA Ops:
  77.1 3.2 %copy-start.1 = (bf16[256,512]{1,0:T(8,128)(2,1)S(1)}, bf16[256,512]{1,0:T(8,128)(2,1)}, u32[]{:S(2)}) copy-start(bf16[256,512]{1,0:T(8,128)(2,1)} %get-tuple-element.9) | copy-start | bytes 786436
  77.1 3.9 %copy-start = (bf16[256,512]{1,0:T(8,128)(2,1)S(1)}, bf16[256,512]{1,0:T(8,128)(2,1)}, u32[]{:S(2)}) copy-start(bf16[256,512]{1,0:T(8,128)(2,1)} %get-tuple-element.10) | copy-start | bytes 786436

commit v2 on v1

v2 whole, which is shorter than its diff:
```python
import functools

import jax
import jax.numpy as jnp
from jax import lax
from jax.experimental import pallas as pl
from jax.experimental.pallas import tpu as pltpu
from jax.sharding import PartitionSpec as P

HD = 128
BLOCK = 128
MOST = 6
DOMAINS = 22
SCALE = HD**-0.5
LOG2E = 1.4426950408889634
HIDDEN = -1e30
HALO = (MOST - 1) * BLOCK
WINDOW = MOST * BLOCK
NT = (((1,), (1,)), ((), ()))
NN = (((1,), (0,)), ((), ()))
MESH = pl.DeviceIdType.MESH
f32 = jnp.float32
bf16 = jnp.bfloat16


def dot(a, b, dims):
    return lax.dot_general(a, b, dims, preferred_element_type=f32)


def kernel(
    n_ctx, n_dp, groups, per_group,
    blocks_ref, domain_ref, weight_ref, q_hbm, k_hbm, v_hbm, t_hbm,
    gq_ref, gk_ref, gv_ref, loss_ref,
    qv, tv, tT, kv, kT, vT, raised, gout, center, acc, own, keep, sbuf, rbuf, lossv, lsend, lrecv, tri,
    kv_sem, q_sem, t_sem, halo_send, halo_recv, grad_send, grad_recv, l_send, l_recv,
):
    me = lax.axis_index("ctx")
    my_dp = lax.axis_index("dp")
    rows = 2 * BLOCK
    heads_w = per_group * HD

    def kv_copy(g, which):
        src = (k_hbm, v_hbm)[which]
        return pltpu.make_async_copy(
            src.at[:, pl.ds(pl.multiple_of(g * HD, HD), HD)],
            kv.at[g, which, pl.ds(HALO, rows), :],
            kv_sem.at[g, which],
        )

    def wide(ref, g):
        return ref.at[:, pl.ds(pl.multiple_of(g * heads_w, heads_w), heads_w)]

    def q_copy(g):
        return pltpu.make_async_copy(wide(q_hbm, g), wide(qv, g), q_sem.at[g])

    def t_copy(g):
        return pltpu.make_async_copy(wide(t_hbm, g), wide(tv, g), t_sem.at[g])

    halos = ((1, HALO, HALO - rows, rows), (3, HALO + BLOCK, 0, BLOCK), (1, HALO - rows, BLOCK, BLOCK), (-1, 0, 2 * BLOCK, BLOCK), (2, HALO, BLOCK, rows))

    def halo_copy(g, i):
        ahead, first, there, count = halos[i]
        return pltpu.make_async_remote_copy(
            src_ref=kv.at[g, :, pl.ds(first, count), :],
            dst_ref=kv.at[g, :, pl.ds(there, count), :],
            send_sem=halo_send.at[g, i],
            recv_sem=halo_recv.at[g, i],
            device_id={"ctx": lax.rem(me + (n_ctx + ahead), n_ctx)},
            device_id_type=MESH,
        )


    def grad_copy(g, i):
        steps = (-1, 1, -1, -1, -3)[i]
        return pltpu.make_async_remote_copy(
            src_ref=sbuf.at[g, i],
            dst_ref=rbuf.at[g, i],
            send_sem=grad_send.at[g, i],
            recv_sem=grad_recv.at[g, i],
            device_id={"ctx": lax.rem(me + (n_ctx + steps), n_ctx)},
            device_id_type=MESH,
        )

    def loss_copy(phase, i):
        if phase == 0:
            slot, target = me, {"ctx": lax.rem(me + i, n_ctx)}
        else:
            slot, target = my_dp, {"dp": lax.rem(my_dp + i, n_dp)}
        return pltpu.make_async_remote_copy(
            src_ref=lsend.at[phase],
            dst_ref=lrecv.at[phase, slot],
            send_sem=l_send.at[phase, i],
            recv_sem=l_recv.at[phase, i],
            device_id=target,
            device_id_type=MESH,
        )

    barrier = pltpu.get_barrier_semaphore()
    for i in range(1, n_ctx):
        pl.semaphore_signal(barrier, inc=1, device_id={"ctx": lax.rem(me + i, n_ctx)}, device_id_type=MESH)
    for i in range(1, n_dp):
        pl.semaphore_signal(barrier, inc=1, device_id={"dp": lax.rem(my_dp + i, n_dp)}, device_id_type=MESH)
    for g in range(groups):
        kv_copy(g, 0).start()
        kv_copy(g, 1).start()
    for g in range(groups):
        q_copy(g).start()
        t_copy(g).start()

    first_block = [2 * me, 2 * me + 1]
    doc_count = blocks_ref.shape[1]
    starts, omegas, domains = [], [], []
    for b in range(2):
        end = jnp.int32(0)
        start = jnp.int32(0)
        doc = jnp.int32(0)
        for i in range(doc_count - 1):
            end = end + blocks_ref[0, i]
            passed = first_block[b] >= end
            start = jnp.where(passed, end, start)
            doc = doc + jnp.where(passed, 1, 0)
        domain = domain_ref[0, doc]
        starts.append(start)
        domains.append(domain)
        omegas.append(weight_ref[domain])
    bias = [
        [jnp.where(first_block[b] - (MOST - 1) + j >= starts[b], 0.0, HIDDEN).astype(f32) for j in range(MOST - 1)]
        for b in range(2)
    ]
    key_row = lax.broadcasted_iota(jnp.int32, (BLOCK, heads_w), 0)
    query_col = lax.rem(lax.broadcasted_iota(jnp.int32, (BLOCK, heads_w), 1), BLOCK)
    tri[...] = jnp.where(key_row <= query_col, 0.0, HIDDEN).astype(f32)
    lossv[...] = jnp.zeros_like(lossv)

    def send_halo(g):
        kv_copy(g, 0).wait()
        kv_copy(g, 1).wait()
        halo_copy(g, 0).start()
        halo_copy(g, 1).start()

    def relay_halo(g):
        halo_copy(g, 0).wait_recv()
        halo_copy(g, 1).wait_recv()
        halo_copy(g, 2).start()
        halo_copy(g, 3).start()

    def send_grads(g):
        for which in range(2):
            sbuf[g, 0, which] = acc[which, BLOCK : 2 * BLOCK, :].astype(bf16)
            sbuf[g, 1, which] = acc[which, 2 * BLOCK : 3 * BLOCK, :].astype(bf16)
            sbuf[g, 2, which] = acc[which, 4 * BLOCK : HALO, :].astype(bf16)
        for i in range(3):
            grad_copy(g, i).start()

        for which in range(2):
            keep[g % 2, 0, which] = acc[which, 3 * BLOCK : 4 * BLOCK, :]
            keep[g % 2, 1, which] = acc[which, 0:BLOCK, :]

        for which in range(2):
            own[g, which] = acc[which, HALO:, :]

    def relay_grads(g):
        for i in range(2):
            grad_copy(g, i).wait_recv()
            for which in range(2):
                sbuf[g, 3 + i, which] = (keep[g % 2, i, which] + rbuf[g, i, which].astype(f32)).astype(bf16)
            grad_copy(g, 3 + i).start()

    def finish(g):
        for i in range(2, 5):
            grad_copy(g, i).wait_recv()
        lanes = pl.ds(pl.multiple_of(g * HD, HD), HD)
        for which, out_ref in ((0, gk_ref), (1, gv_ref)):
            total = own[g, which, 0:BLOCK, :] + rbuf[g, 3, which].astype(f32)
            out_ref[0:BLOCK, lanes] = total.astype(bf16)
            total = own[g, which, BLOCK:rows, :] + rbuf[g, 2, which].astype(f32) + rbuf[g, 4, which].astype(f32)
            out_ref[BLOCK:rows, lanes] = total.astype(bf16)

    lane = lax.broadcasted_iota(jnp.int32, (8, HD), 1)
    line = lax.broadcasted_iota(jnp.int32, (8, HD), 0)

    def start_losses(phase, tile):
        lsend[phase] = tile
        lrecv[phase, (me, my_dp)[phase]] = tile
        for i in range(1, (n_ctx, n_dp)[phase]):
            loss_copy(phase, i).start()

    def add_losses(phase):
        n = (n_ctx, n_dp)[phase]
        for i in range(1, n):
            loss_copy(phase, i).wait()
        tile = lrecv[phase, 0]
        for i in range(1, n):
            tile = tile + lrecv[phase, i]
        return tile

    def slab_losses():
        tile = jnp.zeros((8, HD), f32)
        for b in range(2):
            block_loss = 0.5 * jnp.sum(jnp.sum(lossv[b], axis=0, keepdims=True), axis=1, keepdims=True)
            picked = jnp.where(line == 0, block_loss, jnp.where(line == 1, float(BLOCK), 0.0))
            tile = tile + jnp.where(lane == domains[b], picked, 0.0)
        start_losses(0, tile)

    def turn_targets():
        def turn(g, carry):
            t_copy(g).wait()
            for b in range(2):
                for h in range(per_group):
                    columns = pl.ds(pl.multiple_of(g * heads_w + h * HD, HD), HD)
                    tT[g, b, :, HD * h : HD * (h + 1)] = tv[BLOCK * b : BLOCK * (b + 1), columns].T
            return carry

        lax.fori_loop(0, groups, turn, 0)

    def columns(g, h):
        return pl.ds(pl.multiple_of(g * heads_w + h * HD, HD), HD)

    def queries_of(g, b):
        first = BLOCK * b
        return jnp.concatenate([qv[first : first + BLOCK, columns(g, h)] for h in range(per_group)], 0)

    def forward(g, slot):
        @pl.when(g == 0)
        def _():
            for i in (0, 1, 4):
                halo_copy(0, i).wait_recv()

        @pl.when(g > 0)
        def _():
            halo_copy(g, 2).wait_recv()
            halo_copy(g, 3).wait_recv()

        q_copy(g).wait()
        kT[slot] = kv[g, 0].T
        vT[...] = kv[g, 1].T
        for b in range(2):
            first = BLOCK * b
            scores = dot(kv[g, 0, first : first + WINDOW, :], queries_of(g, b), NT)
            parts, top = [], None
            for j in range(MOST):
                part = scores[BLOCK * j : BLOCK * (j + 1)]
                if j == MOST - 1:
                    part = part + tri[...]
                parts.append(part)
                part_top = jnp.max(part.reshape(BLOCK // 8, 8, heads_w), axis=0)
                if j < MOST - 1:
                    part_top = part_top + bias[b][j]
                top = part_top if top is None else jnp.maximum(top, part_top)
            shift = jnp.max(top, axis=0, keepdims=True) * (SCALE * LOG2E)
            raised_low, sums = [], None
            for j in range(MOST):
                off = shift if j == MOST - 1 else shift - bias[b][j]
                part = jnp.exp2(parts[j] * (SCALE * LOG2E) - off)
                raised_low.append(part.astype(bf16))
                part_sum = jnp.sum(part.reshape(BLOCK // 8, 8, heads_w), axis=0)
                sums = part_sum if sums is None else sums + part_sum
            inverse = 1.0 / jnp.sum(sums, axis=0, keepdims=True)
            raised_low = jnp.concatenate(raised_low, 0)
            raised[slot, b] = raised_low
            out = dot(vT[:, first : first + WINDOW], raised_low, NN) * inverse
            error = out - tT[g, b].astype(f32)
            squares = error * error
            lossv[b] += jnp.sum(squares.reshape(HD // 8, 8, heads_w), axis=0)
            grad_out = (error * (inverse * omegas[b])).astype(bf16)
            gout[slot, b] = grad_out
            center[slot, b] = jnp.sum(grad_out.astype(f32) * out, axis=0, keepdims=True)

    def backward(g, slot, between):
        grad_scores = []
        for b in range(2):
            first = BLOCK * b
            grad_out = gout[slot, b]
            grad_probs = dot(kv[g, 1, first : first + WINDOW, :], grad_out, NN)
            grad_score = (raised[slot, b].astype(f32) * (grad_probs - center[slot, b])).astype(bf16)
            grad_scores.append(grad_score)
            grad_value = dot(raised[slot, b], grad_out, NT)
            grad_key = dot(grad_score, queries_of(g, b), NN) * SCALE
            for which, part in ((0, grad_key), (1, grad_value)):
                if b == 0:
                    acc[which, 0:WINDOW, :] = part
                else:
                    acc[which, BLOCK:WINDOW, :] += part[0 : WINDOW - BLOCK]
                    acc[which, WINDOW:, :] = part[WINDOW - BLOCK :]
        between()
        send_grads(g)
        for b in range(2):
            first = BLOCK * b
            grad_query = dot(kT[slot, :, first : first + WINDOW], grad_scores[b], NN) * SCALE
            for h in range(per_group):
                gq_ref[first : first + BLOCK, columns(g, h)] = grad_query[:, HD * h : HD * (h + 1)].T.astype(bf16)

    def first_groups(g, carry):
        forward(g, 0)

        @pl.when(g == 0)
        def _():
            relay_halo(1)
            send_halo(2)
            send_halo(3)

        @pl.when(g == 1)
        def _():
            relay_halo(2)
            relay_halo(3)

        def between():
            @pl.when(g == 1)
            def _():
                relay_grads(0)

        backward(g, 0, between)
        return carry

    def last_forward(i, carry):
        forward(2 + i, i)
        return carry

    def last_backward(i, carry):
        def between():
            @pl.when(i == 0)
            def _():
                finish(0)

            @pl.when(i == 1)
            def _():
                start_losses(1, add_losses(0))

        backward(2 + i, i, between)
        return carry

    pl.semaphore_wait(barrier, n_ctx - 1 + n_dp - 1)
    send_halo(0)
    halo_copy(0, 4).start()
    send_halo(1)
    turn_targets()
    lax.fori_loop(0, 2, first_groups, 0)
    lax.fori_loop(0, 2, last_forward, 0)
    slab_losses()
    relay_grads(1)
    lax.fori_loop(0, 2, last_backward, 0)
    relay_grads(2)
    finish(1)
    relay_grads(3)
    finish(2)
    finish(3)
    tile = add_losses(1)
    loss_ref[...] = tile[0:1] / (jnp.maximum(tile[1:2], 1.0) * float(groups * per_group * HD))
    for g in range(groups):
        for i in (0, 1, 4) if g == 0 else (0, 1, 2, 3):
            halo_copy(g, i).wait_send()
        for i in range(5):
            grad_copy(g, i).wait_send()


def write(gq_ref, gk_ref, gv_ref, loss_ref, gq_hbm, gk_hbm, gv_hbm, loss_out, sems):
    pairs = ((gq_ref, gq_hbm), (gk_ref, gk_hbm), (gv_ref, gv_hbm))
    copies = [pltpu.make_async_copy(src, dst, sems.at[i]) for i, (src, dst) in enumerate(pairs)]
    for copy in copies:
        copy.start()
    loss_out[...] = loss_ref[0, 0:DOMAINS]
    for copy in copies:
        copy.wait()


def on_device(n_ctx, n_dp, queries, key_states, value_states, targets, doc_blocks, doc_domain, domain_weight):
    rows, q_width = queries.shape[1:]
    kv_width = key_states.shape[2]
    groups = kv_width // HD
    per_group = q_width // kv_width
    heads_w = per_group * HD
    any_space = pl.BlockSpec(memory_space=pl.ANY)
    smem = pl.BlockSpec(memory_space=pltpu.SMEM)
    vmem = pl.BlockSpec(memory_space=pltpu.VMEM)
    dma = pltpu.SemaphoreType.DMA
    span = HALO + rows
    most_peers = max(n_ctx, n_dp)
    gq, gk, gv, loss = pl.pallas_call(
        functools.partial(kernel, n_ctx, n_dp, groups, per_group),
        out_shape=(
            pltpu.VMEM((rows, q_width), bf16),
            pltpu.VMEM((rows, kv_width), bf16),
            pltpu.VMEM((rows, kv_width), bf16),
            pltpu.VMEM((1, HD), f32),
        ),
        in_specs=[smem, smem, smem, any_space, any_space, any_space, any_space],
        out_specs=(vmem,) * 4,
        scratch_shapes=[
            pltpu.VMEM((rows, q_width), bf16),
            pltpu.VMEM((rows, q_width), bf16),
            pltpu.VMEM((groups, 2, HD, heads_w), bf16),
            pltpu.VMEM((groups, 2, span, HD), bf16),
            pltpu.VMEM((2, HD, span), bf16),
            pltpu.VMEM((HD, span), bf16),
            pltpu.VMEM((2, 2, WINDOW, heads_w), bf16),
            pltpu.VMEM((2, 2, HD, heads_w), bf16),
            pltpu.VMEM((2, 2, 1, heads_w), f32),
            pltpu.VMEM((2, span, HD), f32),
            pltpu.VMEM((groups, 2, rows, HD), f32),
            pltpu.VMEM((2, 2, 2, BLOCK, HD), f32),
            pltpu.VMEM((groups, 5, 2, BLOCK, HD), bf16),
            pltpu.VMEM((groups, 5, 2, BLOCK, HD), bf16),
            pltpu.VMEM((2, 8, heads_w), f32),
            pltpu.VMEM((2, 8, HD), f32),
            pltpu.VMEM((2, most_peers, 8, HD), f32),
            pltpu.VMEM((BLOCK, heads_w), f32),
            dma((groups, 2)),
            dma((groups,)),
            dma((groups,)),
            dma((groups, 5)),
            dma((groups, 5)),
            dma((groups, 5)),
            dma((groups, 5)),
            dma((2, most_peers)),
            dma((2, most_peers)),
        ],
        compiler_params=pltpu.CompilerParams(collective_id=0, has_side_effects=True, vmem_limit_bytes=56 << 20),
    )(doc_blocks, doc_domain, domain_weight, queries[0], key_states[0], value_states[0], targets[0])
    gq, gk, gv, loss = pl.pallas_call(
        write,
        out_shape=(
            jax.ShapeDtypeStruct((rows, q_width), bf16),
            jax.ShapeDtypeStruct((rows, kv_width), bf16),
            jax.ShapeDtypeStruct((rows, kv_width), bf16),
            jax.ShapeDtypeStruct((DOMAINS,), f32),
        ),
        in_specs=[vmem] * 4,
        out_specs=(any_space, any_space, any_space, vmem),
        scratch_shapes=[dma((3,))],
    )(*(pltpu.with_memory_space_constraint(x, pltpu.VMEM) for x in (gq, gk, gv, loss)))
    return gq[None], gk[None], gv[None], loss


def solution(mesh):
    placed = (
        P("dp", "ctx", None),
        P("dp", "ctx", None),
        P("dp", "ctx", None),
        P("dp", "ctx", None),
        P("dp", None),
        P("dp", None),
        P(),
    )
    return jax.shard_map(
        functools.partial(on_device, mesh.shape["ctx"], mesh.shape["dp"]),
        mesh=mesh,
        in_specs=placed,
        out_specs=(P("dp", "ctx", None), P("dp", "ctx", None), P("dp", "ctx", None), P()),
        check_vma=False,
    )
```

time: 81.9 us -> 65.9 us (0.80)
  the two profiles are of different devices: /device:TPU:1 before, /device:TPU:24 now
where the time goes in v2:
time: 65.9 us; the launch traced here: 65.8 us
  Pallas kernels  65.2 us (99%)
    pallas_call x1, Pallas kernels, on_device(): pl.pallas_call(functools.partial(kernel, n_ctx, n_dp, groups, per_group),...  63.2 us
    pallas_call x1, Pallas kernels, on_device(): pl.pallas_call(write, out_shape=(jax.ShapeDtypeStruct((rows, q_width), bf...  2.02 us

profile of v2, /device:TPU:24, one launch (start us, length us, event | category | flops | bytes accessed | tf_op | source)
XLA Modules:
  0.0 65.8 jit_solution(8751624221775535335)
XLA Ops:
  0.6 63.2 %shard_map.102 = (bf16[256,4096]{1,0:T(8,128)(2,1)S(1)}, bf16[256,512]{1,0:T(8,128)(2,1)S(1)}, bf16[256,512]{1,0:T(8,128)(2,1)S(1)}, f32[1,128]{1,0:T(1,128)S(1)}) custom-call(s32[1,8]{1,0:T(1,128)} %blocks_ref.1, s32[1,8]{1,0:T(1,128)} %domain_ref.1, f32[22]{0:T(128)} %weight_ref.1, bf16[256,4096]{1,0:T(8,128)(2,1)} %bitcast.7, bf16[256,512]{1,0:T(8,128)(2,1)} %bitcast.9, ...), custom_call_target="tpu_custom_call" | custom-call | tf_op jit(solution)/shard_map/pallas_call | solution.py:378
  63.8 2.0 %shard_map.103 = (bf16[256,4096]{1,0:T(8,128)(2,1)}, bf16[256,512]{1,0:T(8,128)(2,1)}, bf16[256,512]{1,0:T(8,128)(2,1)}, f32[22]{0:T(128)}) custom-call(bf16[256,4096]{1,0:T(8,128)(2,1)S(1)} %get-tuple-element.12.gq_ref, bf16[256,512]{1,0:T(8,128)(2,1)S(1)} %get-tuple-element.13.gk_ref, bf16[256,512]{1,0:T(8,128)(2,1)S(1)} %get-tuple-element.14.gv_ref, ...), custom_call_target="tpu_custom_call" | custom-call | tf_op jit(solution)/shard_map/pallas_call | solution.py:419

commit v3 on v2

--- a/solution.py
+++ b/solution.py
@@ -56,7 +56,7 @@
     def t_copy(g):
         return pltpu.make_async_copy(wide(t_hbm, g), wide(tv, g), t_sem.at[g])
 
-    halos = ((1, HALO, HALO - rows, rows), (3, HALO + BLOCK, 0, BLOCK), (1, HALO - rows, BLOCK, BLOCK), (-1, 0, 2 * BLOCK, BLOCK), (2, HALO, BLOCK, rows))
+    halos = ((1, HALO, HALO - rows, rows), (3, HALO + BLOCK, 0, BLOCK), (1, HALO - rows, BLOCK, BLOCK), (-1, 0, 2 * BLOCK, BLOCK), (2, HALO, BLOCK, BLOCK))
 
     def halo_copy(g, i):
         ahead, first, there, count = halos[i]
@@ -223,7 +223,7 @@
     def forward(g, slot):
         @pl.when(g == 0)
         def _():
-            for i in (0, 1, 4):
+            for i in (0, 3, 4):
                 halo_copy(0, i).wait_recv()
 
         @pl.when(g > 0)
@@ -334,6 +334,8 @@
     halo_copy(0, 4).start()
     send_halo(1)
     turn_targets()
+    halo_copy(0, 1).wait_recv()
+    halo_copy(0, 3).start()
     lax.fori_loop(0, 2, first_groups, 0)
     lax.fori_loop(0, 2, last_forward, 0)
     slab_losses()
@@ -347,7 +349,7 @@
     tile = add_losses(1)
     loss_ref[...] = tile[0:1] / (jnp.maximum(tile[1:2], 1.0) * float(groups * per_group * HD))
     for g in range(groups):
-        for i in (0, 1, 4) if g == 0 else (0, 1, 2, 3):
+        for i in (0, 1, 3, 4) if g == 0 else (0, 1, 2, 3):
             halo_copy(g, i).wait_send()
         for i in range(5):
             grad_copy(g, i).wait_send()

time: 65.9 us -> 63.9 us (0.970)
  Pallas kernels: 65.2 us -> 63.2 us
    pallas_call x1, Pallas kernels: 63.2 us -> 61.2 us  [on_device(): pl.pallas_call(functools.partial(kernel, n_ctx, n_dp, groups, per_group),...]
where the time goes in v3:
time: 63.9 us; the launch traced here: 63.8 us
  Pallas kernels  63.2 us (99%)
  between operations  0.64 us (1%)
    pallas_call x1, Pallas kernels, on_device(): pl.pallas_call(functools.partial(kernel, n_ctx, n_dp, groups, per_group),...  61.2 us
    pallas_call x1, Pallas kernels, on_device(): pl.pallas_call(write, out_shape=(jax.ShapeDtypeStruct((rows, q_width), bf...  2.02 us

profile of v3, /device:TPU:24, one launch (start us, length us, event | category | flops | bytes accessed | tf_op | source)
XLA Modules:
  0.0 63.8 jit_solution(2048136509559318508)
XLA Ops:
  0.6 61.2 %shard_map.102 = (bf16[256,4096]{1,0:T(8,128)(2,1)S(1)}, bf16[256,512]{1,0:T(8,128)(2,1)S(1)}, bf16[256,512]{1,0:T(8,128)(2,1)S(1)}, f32[1,128]{1,0:T(1,128)S(1)}) custom-call(s32[1,8]{1,0:T(1,128)} %blocks_ref.1, s32[1,8]{1,0:T(1,128)} %domain_ref.1, f32[22]{0:T(128)} %weight_ref.1, bf16[256,4096]{1,0:T(8,128)(2,1)} %bitcast.7, bf16[256,512]{1,0:T(8,128)(2,1)} %bitcast.9, ...), custom_call_target="tpu_custom_call" | custom-call | tf_op jit(solution)/shard_map/pallas_call | solution.py:380
  61.8 2.0 %shard_map.103 = (bf16[256,4096]{1,0:T(8,128)(2,1)}, bf16[256,512]{1,0:T(8,128)(2,1)}, bf16[256,512]{1,0:T(8,128)(2,1)}, f32[22]{0:T(128)}) custom-call(bf16[256,4096]{1,0:T(8,128)(2,1)S(1)} %get-tuple-element.12.gq_ref, bf16[256,512]{1,0:T(8,128)(2,1)S(1)} %get-tuple-element.13.gk_ref, bf16[256,512]{1,0:T(8,128)(2,1)S(1)} %get-tuple-element.14.gv_ref, ...), custom_call_target="tpu_custom_call" | custom-call | tf_op jit(solution)/shard_map/pallas_call | solution.py:421
